TPU v7x, 32 devices: a whole 2x2x4 slice. The times are simulated.
32 devices in a mesh: row: 4 (over z), col: 4 (over x, core), tm: 2 (over y).
Axes of the slice: x: 2, y: 2, z: 4, core: 2. Of those that a mesh axis runs over, the one named last changes fastest.
Arguments:
- samples: bfloat16 [1024, 4, 2, 16384], P('row', None, 'tm', 'col'), may hold values from -6 to 6
- whitening: bfloat16 [1024, 1024], replicated, may hold values from -0.1875 to 0.1875
- ridge: float32 [2048], P('col'), may hold values from 2 to 20
- slab_start: int32 [1], replicated, may hold values from 0 to 63
- panels: int32 [4], replicated, may hold values from 0 to 3, as said below
Outputs:
- trailing: float32 [131072, 2048], P(('row', 'tm'), 'col')
- factor: bfloat16 [2, 131072, 512], P(None, ('row', 'tm'))
Inputs may be any that keep to these rules, and one draw needn't show every extreme that they name: `panels`: each panel index once.
All inputs are finite; a program needn't handle non-finite values.
Results may differ from a plain program's by a relative error of at most 0.012.
The roundings to bfloat16 on the way count: a program that leaves them out, or rounds other values in their place, can miss the bound.
Values may be sent and summed in bfloat16 or wider, within the bound.
A program may use at most 256 MiB of HBM per device.

v0:
```python
import jax
import jax.numpy as jnp
from jax import lax
from jax.sharding import PartitionSpec as P

S = 1024
PANEL = 512
PANELS = 2


def broadcast(block, axis, holder):
    block = jnp.where(lax.axis_index(axis) == holder, block, jnp.zeros_like(block))
    return lax.psum(block, axis)


def on_device(samples, whitening, ridge, slab_start, panels):
    moved = lax.all_to_all(samples, "row", split_axis=1, concat_axis=0, tiled=True)
    local_width = moved.shape[3]
    series = moved.reshape(moved.shape[0], local_width)
    whitened = jnp.dot(whitening, series, preferred_element_type=jnp.float32).astype(jnp.bfloat16)
    col_count = lax.axis_size("col")
    tm_count = lax.axis_size("tm")
    rows_here = col_count * local_width
    slab_width = PANEL * col_count
    scale = S ** (-0.5)
    slab_first = slab_start[0] * slab_width
    owner_index = slab_first // rows_here
    slab_offset = slab_first % rows_here
    col_index = lax.axis_index("col")
    self_index = lax.axis_index("row") * tm_count + lax.axis_index("tm")
    row_series = lax.all_gather(whitened, "col", axis=1, tiled=True)
    piece = lax.dynamic_slice_in_dim(row_series, slab_offset + col_index * PANEL, PANEL, 1)
    slab_part = broadcast(piece, ("row", "tm"), owner_index)
    covariance = (
        lax.dot_general(
            row_series, slab_part, (((0,), (0,)), ((), ())), preferred_element_type=jnp.float32
        )
        * scale
    )
    owner_flag = (self_index == owner_index).astype(jnp.float32)
    ridge_rows = slab_offset + col_index * PANEL
    zero_index = jnp.zeros((), jnp.int32)
    diag_block = (
        lax.dynamic_slice(covariance, (ridge_rows, zero_index), (PANEL, PANEL))
        + jnp.diag(ridge) * owner_flag
    )
    covariance = lax.dynamic_update_slice(covariance, diag_block, (ridge_rows, zero_index))
    identity = jnp.eye(PANEL, dtype=jnp.float32)
    factors = []
    finished = col_index < 0
    for section in range(PANELS):
        panel_index = panels[section]
        finished = finished | (col_index == panel_index)
        pivot_local = lax.dynamic_slice_in_dim(
            covariance, slab_offset + panel_index * PANEL, PANEL, 0
        )
        pivot_rows = broadcast(pivot_local, ("row", "tm"), owner_index)
        pivot_safe = jnp.where(col_index == panel_index, pivot_rows, identity)
        lower_factor = jnp.linalg.cholesky(pivot_safe)
        panel_now = jax.scipy.linalg.solve_triangular(lower_factor, covariance.T, lower=True).T
        small_block = lower_factor
        panel_bf = broadcast(panel_now.astype(jnp.bfloat16), "col", panel_index)
        small_block = broadcast(small_block, "col", panel_index)
        coupling = jax.scipy.linalg.solve_triangular(small_block, pivot_rows, lower=True).T
        coupling_bf = coupling.astype(jnp.bfloat16)
        covariance = covariance - lax.dot_general(
            panel_bf, coupling_bf, (((1,), (1,)), ((), ())), preferred_element_type=jnp.float32
        )
        factors.append(panel_bf)
    trailing = jnp.where(finished, jnp.zeros_like(covariance), covariance)
    return (trailing, jnp.stack(factors))


def solution(mesh):
    in_specs = (P("row", None, "tm", "col"), P(), P("col"), P(), P())
    out_specs = (P(("row", "tm"), "col"), P(None, ("row", "tm"), None))
    return jax.shard_map(
        on_device, mesh=mesh, in_specs=in_specs, out_specs=out_specs, check_vma=False
    )
```

profile of v0, /device:TPU:0, one launch (start us, length us, event | category | flops | bytes accessed | tf_op | source)
XLA Modules:
  0.0 1940.5 jit_solution(8248852513893661534)
XLA Ops:
  7.2 11.5 copy.58
  18.7 189.4 %all_to_all.15 = bf16[256,4,1,4096]{3,0,2,1:T(8,128)(2,1)S(1)} all-to-all(bf16[256,4,1,4096]{3,0,2,1:T(8,128)(2,1)} %copy.58), channel_id=1, replica_groups=mesh['row'=4,'col'=4,'tm'=2] {'row'}, dimensions={1} | all-to-all | bytes 16777216 | tf_op jit(solution)/shard_map/all_to_all | solution.py:17
  208.1 10.8 convolution_convert_fusion
  219.7 200.6 %all-gather.2.cloned.1.call-done = bf16[1024,16384]{1,0:T(8,128)(2,1)} async-done(((bf16[1024,4096]{1,0:T(8,128)(2,1)}), bf16[1024,16384]{1,0:T(8,128)(2,1)}) %all-gather.2.cloned.1.call-update) | async-done | bytes 33554448 | tf_op jit(solution)/shard_map/all_gather | solution.py:31
  424.6 78.0 %all-reduce.9.cloned.1.call-done = bf16[1024,512]{1,0:T(8,128)(2,1)} async-done(((bf16[1024,512]{1,0:T(8,128)(2,1)}), bf16[1024,512]{1,0:T(8,128)(2,1)}) %all-reduce.9.cloned.1.call-update) | async-done | bytes 1048592 | tf_op jit(solution)/shard_map/psum | solution.py:13
  502.6 31.8 %convolution_multiply_fusion = f32[16384,512]{0,1:T(8,128)} fusion(bf16[1024,16384]{1,0:T(8,128)(2,1)} %all-gather.2.cloned.1.call-done, bf16[1024,512]{1,0:T(8,128)(2,1)} %all-reduce.9.cloned.1.call-done), kind=kOutput, calls=%fused_computation.12 | convolution fusion | flops 17188257792 | bytes 68157440 | tf_op jit(solution)/shard_map/dot_general | solution.py:35
  545.4 77.0 %all-reduce.11.cloned.1.call-done = f32[512,512]{0,1:T(8,128)} async-done(((f32[512,512]{0,1:T(8,128)}), f32[512,512]{0,1:T(8,128)}) %all-reduce.11.cloned.1.call-update) | async-done | bytes 1048592 | tf_op jit(solution)/shard_map/psum | solution.py:13
  623.1 11.7 cholesky.286
  635.0 9.8 custom-call.31
  645.6 11.7 cholesky.305
  657.4 10.2 custom-call.32
  668.8 11.7 cholesky.326
  680.7 9.8 custom-call.33
  691.3 11.9 cholesky.343
  717.8 39.3 %custom-call.34 = f32[4,128,128]{1,2,0:T(8,128)S(1)} custom-call(f32[4,128,128]{2,1,0:T(8,128)S(1)} %get-tuple-element.33), custom_call_target="InvertDiagBlocksLowerTriangular" | custom-call | tf_op jit(solution)/shard_map/jit(_solve_triangular)/triangular_solve | solution.py:60
  757.2 9.7 fusion.30
  767.0 12.8 convolution_subtract_fusion.4
  789.3 16.7 convolution_subtract_fusion.3
  806.0 11.7 fusion.96
  817.7 22.9 %fusion.15 = f32[128,16384]{1,0:T(8,128)} fusion(f32[128,16384]{1,0:T(8,128)} %fusion.96, f32[128,16384]{1,0:T(8,128)} %fusion.98, f32[128,16384]{1,0:T(8,128)} %copy-done.2, f32[512,16384]{1,0:T(8,128)} %bitcast.173, f32[512,512]{0,1:T(8,128)S(1)} %get-tuple-element.357), kind=kOutput, calls=%fused_computation.31 | convolution fusion | flops 9678356480 | bytes 42139648 | tf_op jit(solution)/shard_map/jit(_solve_triangular)/triangular_solve | solution.py:60
  840.6 11.2 fusion.95
  851.8 17.2 fusion.21
  879.6 39.3 %custom-call.35 = f32[4,128,128]{1,2,0:T(8,128)S(1)} custom-call(f32[4,128,128]{2,1,0:T(8,128)S(1)} %get-tuple-element.34), custom_call_target="InvertDiagBlocksLowerTriangular" | custom-call | tf_op jit(solution)/shard_map/jit(_solve_triangular)/triangular_solve | solution.py:64
  923.8 234.4 %all-reduce.13.cloned.1.call-done = bf16[16384,512]{0,1:T(8,128)(2,1)} async-done(((bf16[16384,512]{0,1:T(8,128)(2,1)}), bf16[16384,512]{0,1:T(8,128)(2,1)}) %all-reduce.13.cloned.1.call-update) | async-done | bytes 16777232 | tf_op jit(solution)/shard_map/psum | solution.py:13
  1158.2 28.8 %convolution_subtract_fusion = f32[16384,512]{0,1:T(8,128)} fusion(f32[16384,512]{0,1:T(8,128)} %dynamic_update_slice.3, bf16[16384,512]{0,1:T(8,128)(2,1)} %all-reduce.13.cloned.1.call-done, bf16[128,512]{1,0:T(8,128)(2,1)S(1)} %fusion.91, f32[128,512]{1,0:T(8,128)S(1)} %fusion.92, f32[128,512]{1,0:T(8,128)S(1)} %fusion.94, f32[128,512]{1,0:T(8,128)S(1)} %fusion.60), kind=kOutput, calls=%fused_computation.25 | convolution fusion | flops 8600420352 | bytes 84803584 | tf_op jit(solution)/shard_map/dot_general | solution.py:66
  1190.5 77.5 %all-reduce.17.cloned.1.call-done = f32[512,512]{0,1:T(8,128)} async-done(((f32[512,512]{0,1:T(8,128)}), f32[512,512]{0,1:T(8,128)}) %all-reduce.17.cloned.1.call-update) | async-done | bytes 1048592 | tf_op jit(solution)/shard_map/psum | solution.py:13
  1268.7 11.7 cholesky.358
  1280.6 9.8 custom-call.36
  1291.2 11.7 cholesky.377
  1303.0 10.3 custom-call.37
  1314.4 11.7 cholesky.398
  1326.3 9.8 custom-call.38
  1336.9 11.8 cholesky.415
  1363.9 39.3 %custom-call.39 = f32[4,128,128]{1,2,0:T(8,128)S(1)} custom-call(f32[4,128,128]{2,1,0:T(8,128)S(1)} %get-tuple-element.35), custom_call_target="InvertDiagBlocksLowerTriangular" | custom-call | tf_op jit(solution)/shard_map/jit(_solve_triangular)/triangular_solve | solution.py:60
  1403.3 9.8 fusion.28
  1413.1 12.8 convolution_subtract_fusion.2
  1425.9 9.5 fusion.88
  1435.4 16.6 convolution_subtract_fusion.1
  1452.0 11.7 fusion.86
  1463.7 22.9 %fusion.12 = f32[128,16384]{1,0:T(8,128)} fusion(f32[128,16384]{1,0:T(8,128)} %fusion.86, f32[128,16384]{1,0:T(8,128)} %fusion.88, f32[128,16384]{1,0:T(8,128)} %copy-done.3, f32[512,16384]{1,0:T(8,128)} %bitcast.169, f32[512,512]{0,1:T(8,128)S(1)} %get-tuple-element.358), kind=kOutput, calls=%fused_computation.30 | convolution fusion | flops 9678356480 | bytes 42139648 | tf_op jit(solution)/shard_map/jit(_solve_triangular)/triangular_solve | solution.py:60
  1486.6 11.2 fusion.85
  1497.8 17.2 fusion.19
  1524.7 39.5 %custom-call.40 = f32[4,128,128]{1,2,0:T(8,128)S(1)} custom-call(f32[4,128,128]{2,1,0:T(8,128)S(1)} %get-tuple-element.36), custom_call_target="InvertDiagBlocksLowerTriangular" | custom-call | tf_op jit(solution)/shard_map/jit(_solve_triangular)/triangular_solve | solution.py:64
  1569.0 234.4 %all-reduce.19.cloned.1.call-done = bf16[16384,512]{0,1:T(8,128)(2,1)} async-done(((bf16[16384,512]{0,1:T(8,128)(2,1)}), bf16[16384,512]{0,1:T(8,128)(2,1)}) %all-reduce.19.cloned.1.call-update) | async-done | bytes 16777232 | tf_op jit(solution)/shard_map/psum | solution.py:13
  1803.4 29.5 %subtract_select_fusion = f32[16384,512]{0,1:T(8,128)} fusion(f32[16384,512]{0,1:T(8,128)} %convolution_subtract_fusion, bf16[16384,512]{0,1:T(8,128)(2,1)} %all-reduce.19.cloned.1.call-done, pred[]{:T(512)S(6)} %or.26, bf16[128,512]{1,0:T(8,128)(2,1)S(1)} %fusion.81, f32[128,512]{1,0:T(8,128)S(1)} %fusion.82, f32[128,512]{1,0:T(8,128)S(1)} %fusion.84, ...), kind=kOutput, calls=%fused_computation.11 | convolution fusion | flops 8608808960 | bytes 84803584 | tf_op jit(solution)/shard_map/dot_general | solution.py:66
  1832.9 33.4 %copy.88 = f32[16384,512]{1,0:T(8,128)} copy(f32[16384,512]{0,1:T(8,128)} %subtract_select_fusion) | data formatting | bytes 67108864
  1866.3 23.0 %pad_maximum_fusion = bf16[2,16384,512]{1,2,0:T(8,128)(2,1)} fusion(bf16[1,16384,512]{1,2,0:T(8,128)(2,1)} %bitcast.175, bf16[1,16384,512]{1,2,0:T(8,128)(2,1)} %bitcast.174), kind=kLoop, calls=%fused_computation.10 | loop fusion | flops 16777216 | bytes 67108864 | tf_op jit(solution)/shard_map/stack | solution.py:71
  1889.3 44.1 %copy.89 = bf16[2,16384,512]{2,1,0:T(8,128)(2,1)} copy(bf16[2,16384,512]{1,2,0:T(8,128)(2,1)} %pad_maximum_fusion) | data formatting | bytes 67108864
  (208 shorter events, 121.2 us)
Async XLA Ops:
  7.2 200.9 %copy-start = (bf16[1024,1024]{1,0:T(8,128)(2,1)S(1)}, bf16[1024,1024]{1,0:T(8,128)(2,1)}, u32[]{:S(2)}) copy-start(bf16[1024,1024]{1,0:T(8,128)(2,1)} %param.11) | copy-start | bytes 6291460
  7.2 413.1 %all-gather.2.cloned.1.call-start = ((), (), s32[]{:S(2)}) async-start(), calls=%async_computation.1 | async-start | bytes 41943040 | tf_op jit(solution)/shard_map/all_gather | solution.py:31
  218.9 204.5 %copy-start.7 = (s32[4]{0:T(128)S(1)}, s32[4]{0:T(128)}, u32[]{:S(2)}) copy-start(s32[4]{0:T(128)} %param.14) | copy-start | bytes 52
  218.9 283.7 %all-reduce.9.cloned.1.call-start = ((), (), s32[]{:S(2)}) async-start(), calls=%async_computation.2 | async-start | bytes 2097152 | tf_op jit(solution)/shard_map/psum | solution.py:13
  423.1 199.3 %all-reduce.11.cloned.1.call-start = ((), (), s32[]{:S(2)}) async-start(), calls=%async_computation.3 | async-start | bytes 2097152 | tf_op jit(solution)/shard_map/psum | solution.py:13
  424.6 109.7 %copy-start.6 = (f32[512]{0:T(512)S(1)}, f32[512]{0:T(512)}, u32[]{:S(2)}) copy-start(f32[512]{0:T(512)} %param.12) | copy-start | bytes 6148
  544.5 325.2 %all-reduce.15.cloned.1.call-start = ((), (), s32[]{:S(2)}) async-start(), calls=%async_computation.5 | async-start | bytes 2097152 | tf_op jit(solution)/shard_map/psum | solution.py:13
  757.2 401.0 %all-reduce.13.cloned.1.call-start = ((), (), s32[]{:S(2)}) async-start(), calls=%async_computation.4 | async-start | bytes 33554432 | tf_op jit(solution)/shard_map/psum | solution.py:13
  767.0 12.8 copy-start.2
  868.9 50.0 %copy-start.4 = (f32[512,512]{0,1:T(8,128)S(1)}, f32[512,512]{0,1:T(8,128)}, u32[]{:S(2)}) copy-start(f32[512,512]{0,1:T(8,128)} %all-reduce.11.cloned.1.call-done) | copy-start | bytes 3145732
  869.0 399.0 %all-reduce.17.cloned.1.call-start = ((), (), s32[]{:S(2)}) async-start(), calls=%async_computation.6 | async-start | bytes 2097152 | tf_op jit(solution)/shard_map/psum | solution.py:13
  1189.6 325.4 %all-reduce.21.cloned.1.call-start = ((), (), s32[]{:S(2)}) async-start(), calls=%async_computation.8 | async-start | bytes 2097152 | tf_op jit(solution)/shard_map/psum | solution.py:13
  1403.2 400.1 %all-reduce.19.cloned.1.call-start = ((), (), s32[]{:S(2)}) async-start(), calls=%async_computation.7 | async-start | bytes 33554432 | tf_op jit(solution)/shard_map/psum | solution.py:13
  1413.0 12.8 copy-start.3
  1515.0 49.2 %copy-start.5 = (f32[512,512]{0,1:T(8,128)S(1)}, f32[512,512]{0,1:T(8,128)}, u32[]{:S(2)}) copy-start(f32[512,512]{0,1:T(8,128)} %all-reduce.17.cloned.1.call-done) | copy-start | bytes 3145732
  1889.3 44.1 %copy-start.1 = (bf16[1024,1024]{1,0:T(8,128)(2,1)S(1)}, bf16[1024,1024]{1,0:T(8,128)(2,1)}, u32[]{:S(2)}) copy-start(bf16[1024,1024]{1,0:T(8,128)(2,1)} %param.11) | copy-start | bytes 6291460
Sparse Core Ops, SparseCore 0:
  219.0 201.1 all-gather.1
  424.3 78.2 all-reduce.8
  544.6 77.7 all-reduce.10
  757.3 37.1 all-reduce.14
  869.1 289.0 all-reduce.12
  1189.7 78.1 all-reduce.16
  1403.4 36.2 all-reduce.20
  1515.1 288.2 all-reduce.18
where the time goes:
time: 1950 us; the launch traced here: 1940 us
  waiting for transfers between devices  902 us (46%)
  other arithmetic  389 us (20%)
  matrix products  304 us (16%)
  blocking collectives  189 us (10%)
  local copies, waits for them, and re-layouts  131 us (7%)
  between operations  23.4 us (1%)
    psum x7, waiting for transfers between devices, broadcast(): return lax.psum(block, axis)  701 us
    all_gather x1, waiting for transfers between devices, on_device(): row_series = lax.all_gather(whitened, 'col', axis=1, tiled=True)  201 us
    all_to_all x1, blocking collectives, on_device(): lax.all_to_all(samples, 'row', split_axis=1, concat_axis=0, tiled=True)  189 us
    another operation x14, matrix products, on_device(): jax.scipy.linalg.solve_triangular(lower_factor, covariance.T, lower=True)  189 us
    another operation x29, other arithmetic, on_device(): lower_factor = jnp.linalg.cholesky(pivot_safe)  159 us
    unnamed x19, local copies, waits for them, and re-layouts  89.1 us
    another operation x4, other arithmetic, on_device(): jax.scipy.linalg.solve_triangular(small_block, pivot_rows, lower=True)  81.5 us
    another operation x3, other arithmetic, on_device(): jax.scipy.linalg.solve_triangular(lower_factor, covariance.T, lower=True)  78.6 us
  transfers between devices with their start and end apart: 8, of which 6 were waited for; matrix products, arithmetic and copies ran while one was open for 17% of the time, Pallas kernels for 0%

commit v1 on v0

--- a/solution.py
+++ b/solution.py
@@ -10,7 +10,7 @@
 
 def broadcast(block, axis, holder):
     block = jnp.where(lax.axis_index(axis) == holder, block, jnp.zeros_like(block))
-    return lax.psum(block, axis)
+    return jnp.sum(lax.all_gather(block, axis), axis=0)
 
 
 def on_device(samples, whitening, ridge, slab_start, panels):

time: 1950 us -> 2680 us (1.37)
  waiting for transfers between devices: 902 us -> 1220 us
  other arithmetic: 389 us -> 593 us
  local copies, waits for them, and re-layouts: 131 us -> 335 us
    all_gather x0 -> x7, waiting for transfers between devices: none -> 1020 us  [broadcast(): return jnp.sum(lax.all_gather(block, axis), axis=0)]
    psum x7 -> x0, waiting for transfers between devices: 701 us -> none  [broadcast(): return lax.psum(block, axis)]
    reduce_sum x0 -> x7, other arithmetic: none -> 207 us  [broadcast(): return jnp.sum(lax.all_gather(block, axis), axis=0)]
    all_gather x0 -> x4, local copies, waits for them, and re-layouts: none -> 181 us  [broadcast(): return jnp.sum(lax.all_gather(block, axis), axis=0)]
    unnamed x19 -> x21, local copies, waits for them, and re-layouts: 89.1 us -> 112 us
  transfers between devices with their start and end apart: 8 -> 8, of which waited for: 6 -> 6; matrix products, arithmetic and copies ran while one was open for 17% -> 13% of each run, Pallas kernels for 0% -> 0%
where the time goes in v1:
time: 2680 us; the launch traced here: 2670 us
  waiting for transfers between devices  1220 us (46%)
  other arithmetic  593 us (22%)
  local copies, waits for them, and re-layouts  335 us (12%)
  matrix products  307 us (11%)
  blocking collectives  189 us (7%)
    all_gather x7, waiting for transfers between devices, broadcast(): return jnp.sum(lax.all_gather(block, axis), axis=0)  1020 us
    reduce_sum x7, other arithmetic, broadcast(): return jnp.sum(lax.all_gather(block, axis), axis=0)  207 us
    all_gather x1, waiting for transfers between devices, on_device(): row_series = lax.all_gather(whitened, 'col', axis=1, tiled=True)  201 us
    all_to_all x1, blocking collectives, on_device(): lax.all_to_all(samples, 'row', split_axis=1, concat_axis=0, tiled=True)  189 us
    another operation x14, matrix products, on_device(): jax.scipy.linalg.solve_triangular(lower_factor, covariance.T, lower=True)  188 us
    all_gather x4, local copies, waits for them, and re-layouts, broadcast(): return jnp.sum(lax.all_gather(block, axis), axis=0)  181 us
    another operation x29, other arithmetic, on_device(): lower_factor = jnp.linalg.cholesky(pivot_safe)  158 us
    unnamed x21, local copies, waits for them, and re-layouts  112 us
  transfers between devices with their start and end apart: 8, of which 6 were waited for; matrix products, arithmetic and copies ran while one was open for 13% of the time, Pallas kernels for 0%

profile of v1, /device:TPU:0, one launch (start us, length us, event | category | flops | bytes accessed | tf_op | source)
XLA Modules:
  0.0 2668.6 jit_solution(18134837151229665901)
XLA Ops:
  7.2 11.5 copy.52
  18.7 189.4 %all_to_all.15 = bf16[256,4,1,4096]{3,0,2,1:T(8,128)(2,1)S(1)} all-to-all(bf16[256,4,1,4096]{3,0,2,1:T(8,128)(2,1)} %copy.52), channel_id=1, replica_groups=mesh['row'=4,'col'=4,'tm'=2] {'row'}, dimensions={1} | all-to-all | bytes 16777216 | tf_op jit(solution)/shard_map/all_to_all | solution.py:17
  208.1 10.8 convolution_convert_fusion
  219.7 200.6 %all-gather.16.cloned.1.call-done = bf16[1024,16384]{1,0:T(8,128)(2,1)} async-done(((bf16[1024,4096]{1,0:T(8,128)(2,1)}), bf16[1024,16384]{1,0:T(8,128)(2,1)}) %all-gather.16.cloned.1.call-update) | async-done | bytes 33554448 | tf_op jit(solution)/shard_map/all_gather | solution.py:31
  424.6 123.2 %all-gather.18.cloned.1.call-done = bf16[8192,512]{1,0:T(8,128)(2,1)} async-done(((bf16[1024,512]{1,0:T(8,128)(2,1)}), bf16[8192,512]{1,0:T(8,128)(2,1)}) %all-gather.18.cloned.1.call-update) | async-done | bytes 8388624 | tf_op jit(solution)/shard_map/all_gather | solution.py:13
  553.0 31.5 %convolution_multiply_fusion = f32[16384,512]{0,1:T(8,128)} fusion(bf16[1024,16384]{1,0:T(8,128)(2,1)} %all-gather.16.cloned.1.call-done, bf16[1024,512]{1,0:T(8,128)(2,1)S(1)} %reduce_sum.72), kind=kOutput, calls=%fused_computation.12 | convolution fusion | flops 17188257792 | bytes 68157440 | tf_op jit(solution)/shard_map/dot_general | solution.py:35
  595.5 122.0 %all-gather.20.cloned.1.call-done = f32[4096,512]{0,1:T(8,128)} async-done(((f32[512,512]{0,1:T(8,128)}), f32[4096,512]{0,1:T(8,128)}) %all-gather.20.cloned.1.call-update) | async-done | bytes 8388624 | tf_op jit(solution)/shard_map/all_gather | solution.py:13
  717.5 11.5 copy.101
  733.2 11.7 cholesky.286
  745.0 9.8 custom-call.31
  755.6 11.8 cholesky.305
  779.4 11.7 cholesky.326
  791.3 9.8 custom-call.33
  802.7 12.1 cholesky.343
  829.8 39.3 %custom-call.34 = f32[4,128,128]{1,2,0:T(8,128)S(1)} custom-call(f32[4,128,128]{2,1,0:T(8,128)S(1)} %get-tuple-element.33), custom_call_target="InvertDiagBlocksLowerTriangular" | custom-call | tf_op jit(solution)/shard_map/jit(_solve_triangular)/triangular_solve | solution.py:60
  878.9 12.8 convolution_subtract_fusion.4
  901.2 16.5 convolution_subtract_fusion.3
  917.8 11.7 fusion.96
  929.5 22.7 fusion.15
  952.2 11.2 fusion.95
  963.4 17.2 fusion.21
  1003.1 39.3 %custom-call.35 = f32[4,128,128]{1,2,0:T(8,128)S(1)} custom-call(f32[4,128,128]{2,1,0:T(8,128)S(1)} %get-tuple-element.34), custom_call_target="InvertDiagBlocksLowerTriangular" | custom-call | tf_op jit(solution)/shard_map/jit(_solve_triangular)/triangular_solve | solution.py:64
  1047.2 324.4 %all-gather.22.cloned.1.call-done = bf16[65536,512]{0,1:T(8,128)(2,1)} async-done(((bf16[16384,512]{0,1:T(8,128)(2,1)}), bf16[65536,512]{0,1:T(8,128)(2,1)}) %all-gather.22.cloned.1.call-update) | async-done | bytes 67108880 | tf_op jit(solution)/shard_map/all_gather | solution.py:13
  1371.6 83.6 %reshape.97 = bf16[4,16384,512]{1,0,2:T(4,128)(2,1)} reshape(bf16[65536,512]{0,1:T(8,128)(2,1)} %all-gather.22.cloned.1.call-done) | data formatting | bytes 134217728 | tf_op jit(solution)/shard_map/all_gather | solution.py:13
  1455.3 91.2 %reduce_sum.74 = bf16[16384,512]{0,1:T(8,128)(2,1)} reduce(bf16[4,16384,512]{1,0,2:T(4,128)(2,1)} %reshape.97, bf16[]{:T(256)} %constant.169.clone.1), dimensions={0}, to_apply=%region_10.13 | reduce | flops 25165824 | bytes 83886080 | tf_op jit(solution)/shard_map/reduce_sum | solution.py:13
  1546.4 28.8 %convolution_subtract_fusion = f32[16384,512]{0,1:T(8,128)} fusion(f32[16384,512]{0,1:T(8,128)} %dynamic_update_slice.3, bf16[16384,512]{0,1:T(8,128)(2,1)} %reduce_sum.74, bf16[128,512]{1,0:T(8,128)(2,1)S(1)} %fusion.91, f32[128,512]{1,0:T(8,128)S(1)} %fusion.92, f32[128,512]{1,0:T(8,128)S(1)} %fusion.94, f32[128,512]{1,0:T(8,128)S(1)} %fusion.60), kind=kOutput, calls=%fused_computation.25 | convolution fusion | flops 8600420352 | bytes 84803584 | tf_op jit(solution)/shard_map/dot_general | solution.py:66
  1578.8 123.7 %all-gather.26.cloned.1.call-done = f32[4096,512]{0,1:T(8,128)} async-done(((f32[512,512]{0,1:T(8,128)}), f32[4096,512]{0,1:T(8,128)}) %all-gather.26.cloned.1.call-update) | async-done | bytes 8388624 | tf_op jit(solution)/shard_map/all_gather | solution.py:13
  1702.5 11.5 copy.102
  1718.2 11.7 cholesky.358
  1730.1 9.8 custom-call.36
  1740.7 11.8 cholesky.377
  1764.5 11.7 cholesky.398
  1787.8 12.1 cholesky.415
  1814.8 39.3 %custom-call.39 = f32[4,128,128]{1,2,0:T(8,128)S(1)} custom-call(f32[4,128,128]{2,1,0:T(8,128)S(1)} %get-tuple-element.35), custom_call_target="InvertDiagBlocksLowerTriangular" | custom-call | tf_op jit(solution)/shard_map/jit(_solve_triangular)/triangular_solve | solution.py:60
  1864.0 12.8 convolution_subtract_fusion.2
  1886.3 16.5 convolution_subtract_fusion.1
  1902.8 11.7 fusion.86
  1914.5 22.7 fusion.12
  1937.2 11.2 fusion.85
  1948.5 17.2 fusion.19
  1987.4 39.3 %custom-call.40 = f32[4,128,128]{1,2,0:T(8,128)S(1)} custom-call(f32[4,128,128]{2,1,0:T(8,128)S(1)} %get-tuple-element.36), custom_call_target="InvertDiagBlocksLowerTriangular" | custom-call | tf_op jit(solution)/shard_map/jit(_solve_triangular)/triangular_solve | solution.py:64
  2031.5 325.2 %all-gather.28.cloned.1.call-done = bf16[65536,512]{0,1:T(8,128)(2,1)} async-done(((bf16[16384,512]{0,1:T(8,128)(2,1)}), bf16[65536,512]{0,1:T(8,128)(2,1)}) %all-gather.28.cloned.1.call-update) | async-done | bytes 67108880 | tf_op jit(solution)/shard_map/all_gather | solution.py:13
  2356.7 83.6 %reshape.100 = bf16[4,16384,512]{1,0,2:T(4,128)(2,1)} reshape(bf16[65536,512]{0,1:T(8,128)(2,1)} %all-gather.28.cloned.1.call-done) | data formatting | bytes 134217728 | tf_op jit(solution)/shard_map/all_gather | solution.py:13
  2440.3 91.2 %reduce_sum.77 = bf16[16384,512]{0,1:T(8,128)(2,1)} reduce(bf16[4,16384,512]{1,0,2:T(4,128)(2,1)} %reshape.100, bf16[]{:T(256)} %constant.169.clone.1), dimensions={0}, to_apply=%region_13.17 | reduce | flops 25165824 | bytes 83886080 | tf_op jit(solution)/shard_map/reduce_sum | solution.py:13
  2531.5 29.5 %subtract_select_fusion = f32[16384,512]{0,1:T(8,128)} fusion(f32[16384,512]{0,1:T(8,128)} %convolution_subtract_fusion, bf16[16384,512]{0,1:T(8,128)(2,1)} %reduce_sum.77, pred[]{:T(512)S(6)} %or.26, bf16[128,512]{1,0:T(8,128)(2,1)S(1)} %fusion.81, f32[128,512]{1,0:T(8,128)S(1)} %fusion.82, f32[128,512]{1,0:T(8,128)S(1)} %fusion.84, f32[128,512]{1,0:T(8,128)S(1)} %fusion.57), kind=kOutput, calls=%fused_computation.11 | convolution fusion | flops 8608808960 | bytes 84803584 | tf_op jit(solution)/shard_map/dot_general | solution.py:66
  2561.0 33.4 %copy.82 = f32[16384,512]{1,0:T(8,128)} copy(f32[16384,512]{0,1:T(8,128)} %subtract_select_fusion) | data formatting | bytes 67108864
  2594.5 23.0 pad_maximum_fusion
  2617.5 44.1 %copy.83 = bf16[2,16384,512]{2,1,0:T(8,128)(2,1)} copy(bf16[2,16384,512]{1,2,0:T(8,128)(2,1)} %pad_maximum_fusion) | data formatting | bytes 67108864
  (221 shorter events, 220.0 us)
Async XLA Ops:
  7.2 200.9 %copy-start = (bf16[1024,1024]{1,0:T(8,128)(2,1)S(1)}, bf16[1024,1024]{1,0:T(8,128)(2,1)}, u32[]{:S(2)}) copy-start(bf16[1024,1024]{1,0:T(8,128)(2,1)} %param.11) | copy-start | bytes 6291460
  7.2 413.1 %all-gather.16.cloned.1.call-start = ((), (), s32[]{:S(2)}) async-start(), calls=%async_computation.1 | async-start | bytes 41943040 | tf_op jit(solution)/shard_map/all_gather | solution.py:31
  218.9 204.5 %copy-start.7 = (s32[4]{0:T(128)S(1)}, s32[4]{0:T(128)}, u32[]{:S(2)}) copy-start(s32[4]{0:T(128)} %param.14) | copy-start | bytes 52
  218.9 328.8 %all-gather.18.cloned.1.call-start = ((), (), s32[]{:S(2)}) async-start(), calls=%async_computation.2 | async-start | bytes 9437184 | tf_op jit(solution)/shard_map/all_gather | solution.py:13
  423.1 294.3 %all-gather.20.cloned.1.call-start = ((), (), s32[]{:S(2)}) async-start(), calls=%async_computation.3 | async-start | bytes 9437184 | tf_op jit(solution)/shard_map/all_gather | solution.py:13
  553.0 31.6 %copy-start.6 = (f32[512]{0:T(512)S(1)}, f32[512]{0:T(512)}, u32[]{:S(2)}) copy-start(f32[512]{0:T(512)} %param.12) | copy-start | bytes 6148
  594.7 386.7 %all-gather.24.cloned.1.call-start = ((), (), s32[]{:S(2)}) async-start(), calls=%async_computation.5 | async-start | bytes 5242880 | tf_op jit(solution)/shard_map/all_gather | solution.py:13
  733.1 34.5 %copy-start.4 = (f32[512,512]{1,0:T(8,128)}, f32[512,512]{1,0:T(8,128)S(1)}, u32[]{:S(2)}) copy-start(f32[512,512]{1,0:T(8,128)S(1)} %fusion.33) | copy-start | bytes 3145732
  869.1 502.5 %all-gather.22.cloned.1.call-start = ((), (), s32[]{:S(2)}) async-start(), calls=%async_computation.4 | async-start | bytes 83886080 | tf_op jit(solution)/shard_map/all_gather | solution.py:13
  878.9 12.8 copy-start.2
  980.6 721.9 %all-gather.26.cloned.1.call-start = ((), (), s32[]{:S(2)}) async-start(), calls=%async_computation.6 | async-start | bytes 9437184 | tf_op jit(solution)/shard_map/all_gather | solution.py:13
  1577.9 387.8 %all-gather.30.cloned.1.call-start = ((), (), s32[]{:S(2)}) async-start(), calls=%async_computation.8 | async-start | bytes 5242880 | tf_op jit(solution)/shard_map/all_gather | solution.py:13
  1718.2 34.5 %copy-start.5 = (f32[512,512]{1,0:T(8,128)}, f32[512,512]{1,0:T(8,128)S(1)}, u32[]{:S(2)}) copy-start(f32[512,512]{1,0:T(8,128)S(1)} %fusion.32) | copy-start | bytes 3145732
  1854.2 502.6 %all-gather.28.cloned.1.call-start = ((), (), s32[]{:S(2)}) async-start(), calls=%async_computation.7 | async-start | bytes 83886080 | tf_op jit(solution)/shard_map/all_gather | solution.py:13
  1864.0 12.8 copy-start.3
  2617.4 44.1 %copy-start.1 = (bf16[1024,1024]{1,0:T(8,128)(2,1)S(1)}, bf16[1024,1024]{1,0:T(8,128)(2,1)}, u32[]{:S(2)}) copy-start(bf16[1024,1024]{1,0:T(8,128)(2,1)} %param.11) | copy-start | bytes 6291460
Sparse Core Ops, SparseCore 0:
  219.0 201.1 all-gather.15
  423.2 124.4 all-gather.17
  594.8 122.6 all-gather.19
  869.2 32.6 all-gather.23
  980.7 390.9 all-gather.21
  1578.0 124.4 all-gather.25
  1854.3 32.6 all-gather.29
  1965.8 390.9 all-gather.27
